TPU v7x, 256 devices: a whole 4x4x8 slice. The times are simulated.
256 devices in a mesh: tm: 32 (over y, z_lo, core), space: 8 (over z_hi, x).
Axes of the slice: x: 4, y: 4, z: 8 (z_hi: 2, z_lo: 4; z = z_hi * 4 + z_lo), core: 2. Of those that a mesh axis runs over, the one named last changes fastest.
Arguments:
- c_points: float32 [64, 3, 256, 512], P('tm', None, 'space'), may hold values from -0.45 to 1.3, as said below
Outputs:
- updated: float32 [64, 3, 256, 512], P('tm', None, 'space')
- coarse_residual: float32 [64, 3, 8, 32, 512], P(None, None, 'space', 'tm')
Inputs may be any that keep to these rules, and one draw needn't show every extreme that they name: `c_points`: the first field (height) lies in 0.7 to 1.3, the other two (momenta) in -0.45 to 0.45.
All inputs are finite; a program needn't handle non-finite values.
Results may differ from a plain program's by a relative error of at most 0.000028.
Values sent between devices are 32-bit elements; how exact they have to be, the bound alone decides.
A program may use at most 64 MiB of HBM per device.

v0:
```python
import jax
import jax.numpy as jnp
from jax import lax
from jax.sharding import PartitionSpec as P

FACTOR = 8


gravity = 1.0
half_ratio = 0.1


def padded(block, sides, width):
    for axis, dim in sides:
        count = lax.axis_size(axis)
        forward = [(i, i + 1) for i in range(count - 1)]
        forward.append((count - 1, 0))
        backward = [(target, source) for source, target in forward]
        low = lax.ppermute(
            lax.slice_in_dim(block, block.shape[dim] - width, None, axis=dim), axis, forward
        )
        high = lax.ppermute(lax.slice_in_dim(block, 0, width, axis=dim), axis, backward)
        block = jnp.concatenate([low, block, high], axis=dim)
    return block


def from_behind(block, axis, distance):
    devices = range(lax.axis_size(axis))
    route = [(i - distance, i) for i in devices if i - distance in devices]
    return lax.ppermute(block, axis, route)


def column_flux(state):
    height = state[..., 0, :, :]
    east_flow = state[..., 1, :, :]
    north_flow = state[..., 2, :, :]
    velocity = east_flow / height
    return jnp.stack(
        [east_flow, east_flow * velocity + 0.5 * gravity * height * height, north_flow * velocity],
        axis=-3,
    )


def row_flux(state):
    height = state[..., 0, :, :]
    east_flow = state[..., 1, :, :]
    north_flow = state[..., 2, :, :]
    velocity = north_flow / height
    return jnp.stack(
        [north_flow, east_flow * velocity, north_flow * velocity + 0.5 * gravity * height * height],
        axis=-3,
    )


def flux_step(extended):
    center = extended[..., 1:-1, :]
    upper_row = extended[..., 2:, :]
    lower_row = extended[..., :-2, :]
    right_cells = jnp.roll(center, -1, axis=-1)
    left_cells = jnp.roll(center, 1, axis=-1)
    average = 0.25 * (upper_row + lower_row + right_cells + left_cells)
    return (
        average
        - half_ratio * (column_flux(right_cells) - column_flux(left_cells))
        - half_ratio * (row_flux(upper_row) - row_flux(lower_row))
    )


def propagate(state):
    extended = padded(state, (("space", 2),), FACTOR)
    for step in range(FACTOR):
        extended = flux_step(extended)
    return extended


def on_device(c_points):
    leading = lax.axis_index("tm") == 0
    advanced = propagate(c_points)
    incoming = from_behind(advanced[-1], "tm", 1)
    opening = jnp.where(leading, c_points[0], incoming)
    updated = jnp.concatenate([opening[None], advanced[:-1]], axis=0)
    pushed = propagate(updated)
    residual = pushed - advanced
    coarse = lax.all_to_all(residual, "tm", split_axis=2, concat_axis=0, tiled=True)
    return (updated, coarse[:, :, None])


def solution(mesh):
    in_specs = (P("tm", None, "space", None),)
    out_specs = (P("tm", None, "space", None), P(None, None, "space", "tm", None))
    return jax.shard_map(
        on_device, mesh=mesh, in_specs=in_specs, out_specs=out_specs, check_vma=False
    )
```

profile of v0, /device:TPU:7, one launch (start us, length us, event | category | flops | bytes accessed | tf_op | source)
XLA Modules:
  0.0 91.4 jit_solution(16181834293415735324)
XLA Ops:
  0.6 1.0 %fusion.388 = (f32[2,3,8,512]{3,2,1,0:T(8,128)S(1)}, f32[2,3,8,512]{3,2,1,0:T(8,128)S(1)}) fusion(f32[2,3,32,512]{3,2,1,0:T(8,128)} %param.1), kind=kLoop, calls=%fused_computation.767 | loop fusion | bytes 393216 | tf_op jit(solution)/shard_map/slice | solution.py:22
  1.6 6.9 %collective-permute-start = (f32[2,3,8,512]{3,2,1,0:T(8,128)S(1)}, f32[2,3,8,512]{3,2,1,0:T(8,128)S(1)}, u32[]{:S(2)}, u32[]{:S(2)}) collective-permute-start(f32[2,3,8,512]{3,2,1,0:T(8,128)S(1)} %get-tuple-element.239), channel_id=1, source_target_pairs={{0,1},{1,2},{2,3},{3,4},{4,5},{5,6},{6,7},{7,0},{8,9},{9,10},{10,1... | collective-permute-start | bytes 294920 | tf_op jit(solution)/shard_map/ppermute | solution.py:19
  8.6 1.6 %collective-permute-done = f32[2,3,8,512]{3,2,1,0:T(8,128)S(1)} collective-permute-done((f32[2,3,8,512]{3,2,1,0:T(8,128)S(1)}, f32[2,3,8,512]{3,2,1,0:T(8,128)S(1)}, u32[]{:S(2)}, u32[]{:S(2)}) %collective-permute-start) | collective-permute-done | bytes 98336 | tf_op jit(solution)/shard_map/ppermute | solution.py:19
  10.2 7.9 %collective-permute-done.1 = f32[2,3,8,512]{3,2,1,0:T(8,128)S(1)} collective-permute-done((f32[2,3,8,512]{3,2,1,0:T(8,128)S(1)}, f32[2,3,8,512]{3,2,1,0:T(8,128)S(1)}, u32[]{:S(2)}, u32[]{:S(2)}) %collective-permute-start.1) | collective-permute-done | bytes 98336 | tf_op jit(solution)/shard_map/ppermute | solution.py:22
  19.2 0.6 fusion.28
  20.9 0.6 fusion.23
  22.6 0.6 fusion.18
  24.2 0.5 fusion.80
  30.3 6.5 %collective-permute-start.2 = (f32[3,32,512]{2,1,0:T(8,128)S(1)}, f32[3,32,512]{2,1,0:T(8,128)S(1)}, u32[]{:S(2)}, u32[]{:S(2)}) collective-permute-start(f32[3,32,512]{2,1,0:T(8,128)S(1)} %get-tuple-element.236), channel_id=1, source_target_pairs={{0,8},{8,16},{16,24},{24,32},{32,40},{40,48},{48,56},{56,64},{64,7... | collective-permute-start | bytes 589832 | tf_op jit(solution)/shard_map/ppermute | solution.py:30
  36.8 3.8 %collective-permute-done.2 = f32[3,32,512]{2,1,0:T(8,128)S(1)} collective-permute-done((f32[3,32,512]{2,1,0:T(8,128)S(1)}, f32[3,32,512]{2,1,0:T(8,128)S(1)}, u32[]{:S(2)}, u32[]{:S(2)}) %collective-permute-start.2) | collective-permute-done | bytes 196640 | tf_op jit(solution)/shard_map/ppermute | solution.py:30
  40.8 1.5 %collective-permute-start.4 = (f32[2,3,8,512]{3,2,1,0:T(8,128)S(1)}, f32[2,3,8,512]{3,2,1,0:T(8,128)S(1)}, u32[]{:S(2)}, u32[]{:S(2)}) collective-permute-start(f32[2,3,8,512]{3,2,1,0:T(8,128)S(1)} %get-tuple-element.235), channel_id=1, source_target_pairs={{1,0},{2,1},{3,2},{4,3},{5,4},{6,5},{7,6},{0,7},{9,8},{10,9},{11,1... | collective-permute-start | bytes 294920 | tf_op jit(solution)/shard_map/ppermute | solution.py:22
  42.2 2.3 %collective-permute-done.3 = f32[2,3,8,512]{3,2,1,0:T(8,128)S(1)} collective-permute-done((f32[2,3,8,512]{3,2,1,0:T(8,128)S(1)}, f32[2,3,8,512]{3,2,1,0:T(8,128)S(1)}, u32[]{:S(2)}, u32[]{:S(2)}) %collective-permute-start.3) | collective-permute-done | bytes 98336 | tf_op jit(solution)/shard_map/ppermute | solution.py:19
  44.5 7.1 %collective-permute-done.4 = f32[2,3,8,512]{3,2,1,0:T(8,128)S(1)} collective-permute-done((f32[2,3,8,512]{3,2,1,0:T(8,128)S(1)}, f32[2,3,8,512]{3,2,1,0:T(8,128)S(1)}, u32[]{:S(2)}, u32[]{:S(2)}) %collective-permute-start.4) | collective-permute-done | bytes 98336 | tf_op jit(solution)/shard_map/ppermute | solution.py:22
  52.8 0.6 fusion.13
  54.5 0.6 fusion.8
  56.2 0.6 fusion.3
  57.7 0.5 fusion.60
  59.2 0.5 fusion.55
  60.7 0.5 fusion.50
  63.9 1.1 %copy.443 = f32[2,3,32,512]{3,1,0,2:T(4,128)} copy(f32[2,3,32,512]{3,2,1,0:T(8,128)S(1)} %fusion.102) | data formatting | bytes 786432 | tf_op jit(solution)/shard_map/sub | solution.py:83
  65.0 8.5 %all-to-all-start = ((f32[2,3,32,512]{3,1,0,2:T(4,128)}), f32[2,3,32,512]{3,1,0,2:T(4,128)S(1)}, u32[]{:S(2)}, u32[]{:S(2)}) async-start(f32[2,3,32,512]{3,1,0,2:T(4,128)} %copy.443), calls=%async_computation | async-start | bytes 1048576 | tf_op jit(solution)/shard_map/all_to_all | solution.py:84
  73.5 0.8 pad_maximum_fusion.33
  74.3 16.0 %all-to-all-done = f32[2,3,32,512]{3,1,0,2:T(4,128)S(1)} async-done(((f32[2,3,32,512]{3,1,0,2:T(4,128)}), f32[2,3,32,512]{3,1,0,2:T(4,128)S(1)}, u32[]{:S(2)}, u32[]{:S(2)}) %all-to-all-start) | async-done | bytes 393248 | tf_op jit(solution)/shard_map/all_to_all | solution.py:84
  90.3 1.2 %copy.444 = f32[64,3,1,1,512]{4,3,2,1,0:T(1,128)} copy(f32[64,3,1,1,512]{4,1,0,3,2:T(4,128)S(1)} %bitcast.13) | data formatting | bytes 786432
  (128 shorter events, 18.6 us)
Async XLA Ops:
  0.6 9.6 %copy-start = (f32[2,3,32,512]{3,2,1,0:T(8,128)S(1)}, f32[2,3,32,512]{3,2,1,0:T(8,128)}, u32[]{:S(2)}) copy-start(f32[2,3,32,512]{3,2,1,0:T(8,128)} %param.1) | copy-start | bytes 1179652
  1.6 8.5 %collective-permute-start = (f32[2,3,8,512]{3,2,1,0:T(8,128)S(1)}, f32[2,3,8,512]{3,2,1,0:T(8,128)S(1)}, u32[]{:S(2)}, u32[]{:S(2)}) collective-permute-start(f32[2,3,8,512]{3,2,1,0:T(8,128)S(1)} %get-tuple-element.239), channel_id=1, source_target_pairs={{0,1},{1,2},{2,3},{3,4},{4,5},{5,6},{6,7},{7,0},{8,9},{9,10},{10,1... | collective-permute-start | bytes 294920 | tf_op jit(solution)/shard_map/ppermute | solution.py:19
  8.5 9.6 %collective-permute-start.1 = (f32[2,3,8,512]{3,2,1,0:T(8,128)S(1)}, f32[2,3,8,512]{3,2,1,0:T(8,128)S(1)}, u32[]{:S(2)}, u32[]{:S(2)}) collective-permute-start(f32[2,3,8,512]{3,2,1,0:T(8,128)S(1)} %get-tuple-element.238), channel_id=1, source_target_pairs={{1,0},{2,1},{3,2},{4,3},{5,4},{6,5},{7,6},{0,7},{9,8},{10,9},{11,1... | collective-permute-start | bytes 294920 | tf_op jit(solution)/shard_map/ppermute | solution.py:22
  30.3 10.4 %collective-permute-start.2 = (f32[3,32,512]{2,1,0:T(8,128)S(1)}, f32[3,32,512]{2,1,0:T(8,128)S(1)}, u32[]{:S(2)}, u32[]{:S(2)}) collective-permute-start(f32[3,32,512]{2,1,0:T(8,128)S(1)} %get-tuple-element.236), channel_id=1, source_target_pairs={{0,8},{8,16},{16,24},{24,32},{32,40},{40,48},{48,56},{56,64},{64,7... | collective-permute-start | bytes 589832 | tf_op jit(solution)/shard_map/ppermute | solution.py:30
  40.7 3.8 %collective-permute-start.3 = (f32[2,3,8,512]{3,2,1,0:T(8,128)S(1)}, f32[2,3,8,512]{3,2,1,0:T(8,128)S(1)}, u32[]{:S(2)}, u32[]{:S(2)}) collective-permute-start(f32[2,3,8,512]{3,2,1,0:T(8,128)S(1)} %get-tuple-element.234), channel_id=1, source_target_pairs={{0,1},{1,2},{2,3},{3,4},{4,5},{5,6},{6,7},{7,0},{8,9},{9,10},{10,1... | collective-permute-start | bytes 294920 | tf_op jit(solution)/shard_map/ppermute | solution.py:19
  40.8 10.8 %collective-permute-start.4 = (f32[2,3,8,512]{3,2,1,0:T(8,128)S(1)}, f32[2,3,8,512]{3,2,1,0:T(8,128)S(1)}, u32[]{:S(2)}, u32[]{:S(2)}) collective-permute-start(f32[2,3,8,512]{3,2,1,0:T(8,128)S(1)} %get-tuple-element.235), channel_id=1, source_target_pairs={{1,0},{2,1},{3,2},{4,3},{5,4},{6,5},{7,6},{0,7},{9,8},{10,9},{11,1... | collective-permute-start | bytes 294920 | tf_op jit(solution)/shard_map/ppermute | solution.py:22
  65.0 25.3 %all-to-all-start = ((f32[2,3,32,512]{3,1,0,2:T(4,128)}), f32[2,3,32,512]{3,1,0,2:T(4,128)S(1)}, u32[]{:S(2)}, u32[]{:S(2)}) async-start(f32[2,3,32,512]{3,1,0,2:T(4,128)} %copy.443), calls=%async_computation | async-start | bytes 1048576 | tf_op jit(solution)/shard_map/all_to_all | solution.py:84
where the time goes:
time: 91.7 us; the launch traced here: 91.4 us
  waiting for transfers between devices  38.7 us (42%)
  starting transfers between devices  23.5 us (26%)
  other arithmetic  19 us (21%)
  local copies, waits for them, and re-layouts  8.78 us (10%)
  between operations  1.41 us (2%)
    all_to_all x1, waiting for transfers between devices, on_device(): lax.all_to_all(residual, 'tm', split_axis=2, concat_axis=0, tiled=True)  16 us
    ppermute x2, waiting for transfers between devices, padded(): lax.ppermute(lax.slice_in_dim(block, 0, width, axis=dim), axis, backward)  15 us
    all_to_all x1, starting transfers between devices, on_device(): lax.all_to_all(residual, 'tm', split_axis=2, concat_axis=0, tiled=True)  8.51 us
    sub x15, other arithmetic, flux_step(): average - half_ratio * (column_flux(right_cells) - column_flux(left_cells))  7.4 us
    ppermute x2, starting transfers between devices, padded(): lax.ppermute(lax.slice_in_dim(block, block.shape[dim] - width, None, axis...  6.98 us
    ppermute x1, starting transfers between devices, from_behind(): return lax.ppermute(block, axis, route)  6.53 us
    add x31, other arithmetic, column_flux(): east_flow * velocity + 0.5 * gravity * height * height  4.12 us
    mul x32, other arithmetic, column_flux(): north_flow * velocity  4.11 us
  transfers between devices with their start and end apart: 6, of which 6 were waited for; matrix products, arithmetic and copies ran while one was open for 1% of the time, Pallas kernels for 0%

commit v1 on v0

v1 whole, which is shorter than its diff:
```python
import jax
import jax.numpy as jnp
from jax import lax
from jax.experimental import pallas as pl
from jax.experimental.pallas import tpu as pltpu
from jax.sharding import PartitionSpec as P

FACTOR = 8
LANES = 128
HALO = 2 * FACTOR
SUBLANES = 8
MOMENTUM_SCALE = 0.4
SQUARE_SCALE = 0.08
MESH = pl.DeviceIdType.MESH


def inverse(height):
    return 1.0 / height


def step_rows(src, dst, square):
    count = src.shape[1]
    columns = src.shape[3]

    def parts(b):
        h, p, q = src[0, b], src[1, b], src[2, b]
        r = inverse(h)
        u = p * r
        v = q * r
        mixed = u * q
        half = (h * square) * h
        east = u * p + half
        north = v * q + half
        from_east = (h - p, p - east, q - mixed)
        from_west = (h + p, p + east, q + mixed)
        from_north = (h - q, p - mixed, q - north)
        from_south = (h + q, p + mixed, q + north)
        across = [
            pltpu.roll(e, columns - 1, axis=1) + pltpu.roll(w, 1, axis=1)
            for e, w in zip(from_east, from_west)
        ]
        return across, from_north, from_south

    def put(b, across, north, south):
        for f in range(3):
            dst[f, b] = across[f] + (north[f] + south[f])

    first = parts(0)
    second = parts(1)
    older, old = first, second
    for b in range(2, count):
        new = parts(b)
        put(b - 1, old[0], new[1], older[2])
        older, old = old, new
    put(count - 1, old[0], [pltpu.roll(x, SUBLANES - 1, axis=0) for x in first[1]], older[2])
    put(0, first[0], second[1], [pltpu.roll(x, 1, axis=0) for x in old[2]])


def kernel(c_ref, updated, coarse, ext, states, settled, behind, stage,
           local_sem, halo_send, halo_recv, shift_send, shift_recv, row_send, row_recv):
    t = lax.axis_index("tm")
    s = lax.axis_index("space")
    times = lax.axis_size("tm")
    strips = lax.axis_size("space")
    rows, columns = c_ref.shape[2], c_ref.shape[3]
    blocks = columns // LANES
    full = rows + 2 * HALO
    count = full // SUBLANES
    low = lax.rem(s + strips - 1, strips)
    high = lax.rem(s + 1, strips)
    before = lax.rem(t + times - 1, times)
    after = lax.rem(t + 1, times)

    barrier = pltpu.get_barrier_semaphore()

    @pl.loop(1, times)
    def _(d):
        pl.semaphore_signal(barrier, inc=1, device_id=(lax.rem(t + d, times), s), device_id_type=MESH)

    for neighbour in (low, high):
        pl.semaphore_signal(barrier, inc=1, device_id=(t, neighbour), device_id_type=MESH)

    lanes = [pl.ds(i * LANES, LANES) for i in range(blocks)]
    own = [
        [
            pltpu.make_async_copy(
                c_ref.at[k, :, :, lanes[i]], ext.at[k, :, i, pl.ds(HALO, rows), :], local_sem.at[k]
            )
            for i in range(blocks)
        ]
        for k in range(2)
    ]
    for k in range(2):
        for copy in own[k]:
            copy.start()
    opening = pltpu.make_async_copy(c_ref.at[0], updated.at[0], local_sem.at[2])

    @pl.when(t == 0)
    def _():
        opening.start()

    pl.semaphore_wait(barrier, times + 1)

    for k in range(2):
        for i in range(blocks):
            for target, source, place in ((high, rows - HALO, 0), (low, 0, HALO + rows)):
                pltpu.make_async_remote_copy(
                    src_ref=c_ref.at[k, :, pl.ds(source, HALO), lanes[i]],
                    dst_ref=ext.at[k, :, i, pl.ds(place, HALO), :],
                    send_sem=halo_send.at[k],
                    recv_sem=halo_recv.at[k],
                    device_id=(t, target),
                    device_id_type=MESH,
                ).start()

    def halo_bytes(k):
        part = ext.at[k, :, :, pl.ds(0, 2 * HALO), :]
        return pltpu.make_async_remote_copy(
            src_ref=part, dst_ref=part, send_sem=halo_send.at[k], recv_sem=halo_recv.at[k],
            device_id=(t, high), device_id_type=MESH,
        )

    def propagate(k, square):
        a, b = states.at[k, 0], states.at[k, 1]

        def two(_, square):
            step_rows(a, b, square)
            square = square * 0.25
            step_rows(b, a, square)
            return square * 0.25

        return lax.fori_loop(0, FACTOR // 2, two, square)

    down = [0.25 ** (2 * FACTOR), 0.25 ** (2 * FACTOR) / MOMENTUM_SCALE, 0.25 ** (2 * FACTOR) / MOMENTUM_SCALE]
    middle = [0.25 ** FACTOR, 0.25 ** FACTOR / MOMENTUM_SCALE, 0.25 ** FACTOR / MOMENTUM_SCALE]
    square = None
    shifts = []
    for k in range(2):
        part = ext.at[k, :, :, pl.ds(HALO, rows), :]
        pltpu.make_async_copy(part, part, local_sem.at[k]).wait()
        halo_bytes(k).wait_recv()
        for f in range(3):
            for b in range(count):
                for i in range(blocks):
                    value = ext[k, f, i, pl.ds(b, SUBLANES, stride=count), :]
                    if f > 0:
                        value = value * MOMENTUM_SCALE
                    states[k, 0, f, b, :, i * LANES:(i + 1) * LANES] = value
        square = propagate(k, SQUARE_SCALE)
        for f in range(3):
            for b in range(count):
                for i in range(blocks):
                    settled[k, f, i, pl.ds(b, SUBLANES, stride=count), :] = (
                        states[k, 0, f, b, :, i * LANES:(i + 1) * LANES] * middle[f]
                    )
        if k == 0:
            back = pltpu.make_async_remote_copy(
                src_ref=settled.at[0, :, :, pl.ds(HALO, rows), :],
                dst_ref=behind.at[:, :, pl.ds(HALO, rows), :],
                send_sem=shift_send.at[0],
                recv_sem=shift_recv.at[0],
                device_id=(before, s),
                device_id_type=MESH,
            )
            back.start()
            kept = [
                pltpu.make_async_copy(
                    settled.at[0, :, i, pl.ds(HALO, rows), :], updated.at[1, :, :, lanes[i]], local_sem.at[3]
                )
                for i in range(blocks)
            ]
            for copy in kept:
                copy.start()
        else:
            onward = [
                pltpu.make_async_remote_copy(
                    src_ref=settled.at[1, :, i, pl.ds(HALO, rows), :],
                    dst_ref=updated.at[0, :, :, lanes[i]],
                    send_sem=shift_send.at[1],
                    recv_sem=shift_recv.at[1],
                    device_id=(after, s),
                    device_id_type=MESH,
                )
                for i in range(blocks)
            ]

            @pl.when(t < times - 1)
            def _():
                for copy in onward:
                    copy.start()

    def row_copy(k, j):
        interval = lax.rem(2 * t + 1 + k, 2 * times)
        return (
            stage.at[k, pl.ds((HALO + j) * 3, 3)],
            coarse.at[pl.ds(interval * 3, 3)],
        )

    for k in range(2):
        propagate(k, square)
        if k == 1:
            back.wait_recv()
        wrapped = t == times - 1
        for b in range(count):
            for f in range(3):
                for i in range(blocks):
                    value = states[k, 0, f, b, :, i * LANES:(i + 1) * LANES] * down[f]
                    if k == 0:
                        known = settled[1, f, i, pl.ds(b, SUBLANES, stride=count), :]
                    else:
                        known = behind[f, i, pl.ds(b, SUBLANES, stride=count), :]
                        value = jnp.where(wrapped, known, value)
                    stage[k, pl.ds(b * 3 + f, SUBLANES, stride=3 * count), i, :] = value - known

        @pl.loop(1, times)
        def _(d):
            j = lax.rem(t + d, times)
            source, place = row_copy(k, j)
            pltpu.make_async_remote_copy(
                src_ref=source, dst_ref=place, send_sem=row_send.at[k], recv_sem=row_recv.at[k],
                device_id=(j, s), device_id_type=MESH,
            ).start()

        source, place = row_copy(k, t)
        pltpu.make_async_copy(source, place, local_sem.at[4 + k]).start()

    for k in range(2):
        halo_bytes(k).wait_send()
    back.wait_send()
    pltpu.make_async_copy(updated.at[1], updated.at[1], local_sem.at[3]).wait()
    whole = pltpu.make_async_remote_copy(
        src_ref=updated.at[0], dst_ref=updated.at[0], send_sem=shift_send.at[1], recv_sem=shift_recv.at[1],
        device_id=(after, s), device_id_type=MESH,
    )

    @pl.when(t == 0)
    def _():
        opening.wait()

    @pl.when(t > 0)
    def _():
        whole.wait_recv()

    @pl.when(t < times - 1)
    def _():
        whole.wait_send()

    for k in range(2):
        part = coarse.at[pl.ds(0, 3 * (times - 1))]
        total = pltpu.make_async_remote_copy(
            src_ref=part, dst_ref=part, send_sem=row_send.at[k], recv_sem=row_recv.at[k],
            device_id=(after, s), device_id_type=MESH,
        )
        total.wait_recv()
        total.wait_send()
        source, place = row_copy(k, t)
        pltpu.make_async_copy(source, place, local_sem.at[4 + k]).wait()


def solution(mesh):
    def on_device(c_points):
        intervals, fields, rows, columns = c_points.shape
        times = lax.axis_size("tm")
        blocks = columns // LANES
        full = rows + 2 * HALO
        f32 = jnp.float32
        updated, coarse = pl.pallas_call(
            kernel,
            out_shape=(
                jax.ShapeDtypeStruct(c_points.shape, f32),
                jax.ShapeDtypeStruct((2 * times * fields, blocks, LANES), f32),
            ),
            in_specs=[pl.BlockSpec(memory_space=pl.ANY)],
            out_specs=(pl.BlockSpec(memory_space=pl.ANY), pl.BlockSpec(memory_space=pl.ANY)),
            scratch_shapes=[
                pltpu.VMEM((2, fields, blocks, full, LANES), f32),
                pltpu.VMEM((2, 2, fields, full // SUBLANES, SUBLANES, columns), f32),
                pltpu.VMEM((2, fields, blocks, full, LANES), f32),
                pltpu.VMEM((fields, blocks, full, LANES), f32),
                pltpu.VMEM((2, full * fields, blocks, LANES), f32),
                pltpu.SemaphoreType.DMA((6,)),
                pltpu.SemaphoreType.DMA((2,)),
                pltpu.SemaphoreType.DMA((2,)),
                pltpu.SemaphoreType.DMA((2,)),
                pltpu.SemaphoreType.DMA((2,)),
                pltpu.SemaphoreType.DMA((2,)),
                pltpu.SemaphoreType.DMA((2,)),
            ],
            compiler_params=pltpu.CompilerParams(collective_id=0, has_side_effects=True),
        )(c_points)
        return updated, coarse.reshape(2 * times, fields, 1, 1, columns)

    return jax.shard_map(
        on_device,
        mesh=mesh,
        in_specs=(P("tm", None, "space", None),),
        out_specs=(P("tm", None, "space", None), P(None, None, "space", "tm", None)),
        check_vma=False,
    )
```

time: 91.7 us -> 43.4 us (0.47)
  the two profiles are of different devices: /device:TPU:7 before, /device:TPU:1 now
where the time goes in v1:
time: 43.4 us; the launch traced here: 43.3 us
  Pallas kernels  40.1 us (92%)
  local copies, waits for them, and re-layouts  2.58 us (6%)
  between operations  0.65 us (1%)
    pallas_call x1, Pallas kernels, on_device(): pl.pallas_call(kernel, out_shape=(jax.ShapeDtypeStruct(c_points.shape, f3...  40.1 us
    unnamed x4, local copies, waits for them, and re-layouts  2.58 us

profile of v1, /device:TPU:1, one launch (start us, length us, event | category | flops | bytes accessed | tf_op | source)
XLA Modules:
  0.0 43.3 jit_solution(3401865550396410069)
XLA Ops:
  0.6 40.1 %shard_map.30 = (f32[2,3,32,512]{3,2,1,0:T(8,128)}, f32[192,4,128]{2,1,0:T(4,128)}) custom-call(f32[2,3,32,512]{3,2,1,0:T(8,128)} %c_ref.1), custom_call_target="tpu_custom_call" | custom-call | tf_op jit(solution)/shard_map/pallas_call | solution.py:267
  40.7 0.0 copy-start
  40.7 1.8 %copy.7 = f32[2,3,32,512]{3,2,1,0:T(8,128)} copy(f32[2,3,32,512]{3,2,1,0:T(8,128)} %get-tuple-element.12) | data formatting | bytes 786432
  42.5 0.0 copy-done
  42.5 0.7 %copy.8 = f32[64,3,1,1,512]{4,3,2,1,0:T(1,128)} copy(f32[64,3,1,1,512]{4,3,2,1,0:T(1,128)S(1)} %bitcast.1) | data formatting | bytes 786432
Async XLA Ops:
  40.7 1.8 %copy-start = (f32[192,4,128]{2,1,0:T(4,128)S(1)}, f32[192,4,128]{2,1,0:T(4,128)}, u32[]{:S(2)}) copy-start(f32[192,4,128]{2,1,0:T(4,128)} %get-tuple-element.5) | copy-start | bytes 1179652

commit v2 on v1

v2 whole, which is shorter than its diff:
```python
import jax
import jax.numpy as jnp
from jax import lax
from jax.experimental import pallas as pl
from jax.experimental.pallas import tpu as pltpu
from jax.sharding import PartitionSpec as P

FACTOR = 8
LANES = 128
HALO = 2 * FACTOR
SUBLANES = 8
MOMENTUM_SCALE = 0.4
SQUARE_SCALE = 0.08
SCALE_BACK = [0.25 ** FACTOR, 0.25 ** FACTOR / MOMENTUM_SCALE, 0.25 ** FACTOR / MOMENTUM_SCALE]
RUN = 4
MESH = pl.DeviceIdType.MESH


def inverse(height):
    return 1.0 / height


def step_rows(src, dst, square):
    count = src.shape[1]
    columns = src.shape[3]

    def parts(b):
        h, p, q = src[0, b], src[1, b], src[2, b]
        r = inverse(h)
        u = p * r
        v = q * r
        mixed = u * q
        half = (h * square) * h
        east = u * p + half
        north = v * q + half
        from_east = (h - p, p - east, q - mixed)
        from_west = (h + p, p + east, q + mixed)
        from_north = (h - q, p - mixed, q - north)
        from_south = (h + q, p + mixed, q + north)
        across = [
            pltpu.roll(e, columns - 1, axis=1) + pltpu.roll(w, 1, axis=1)
            for e, w in zip(from_east, from_west)
        ]
        return across, from_north, from_south

    def put(b, across, north, south):
        for f in range(3):
            dst[f, b] = across[f] + (north[f] + south[f])

    first = parts(0)
    second = parts(1)
    older, old = first, second
    for b in range(2, count):
        new = parts(b)
        put(b - 1, old[0], new[1], older[2])
        older, old = old, new
    put(count - 1, old[0], [pltpu.roll(x, SUBLANES - 1, axis=0) for x in first[1]], older[2])
    put(0, first[0], second[1], [pltpu.roll(x, 1, axis=0) for x in old[2]])


def kernel(c_ref, updated, coarse, ext, states, settled, behind, stage,
           local_sem, halo_send, halo_recv, back_send, back_recv, on_send, on_recv, row_send, row_recv):
    t = lax.axis_index("tm")
    s = lax.axis_index("space")
    times = lax.axis_size("tm")
    strips = lax.axis_size("space")
    rows, columns = c_ref.shape[2], c_ref.shape[3]
    blocks = columns // LANES
    half = rows // 2
    wide = half + 2 * HALO
    narrow = half + 2 * FACTOR
    low = lax.rem(s + strips - 1, strips)
    high = lax.rem(s + 1, strips)
    before = lax.rem(t + times - 1, times)
    after = lax.rem(t + 1, times)

    barrier = pltpu.get_barrier_semaphore()
    for neighbour in (low, high):
        pl.semaphore_signal(barrier, inc=1, device_id=(t, neighbour), device_id_type=MESH)

    @pl.loop(1, times)
    def _(d):
        pl.semaphore_signal(barrier, inc=1, device_id=(lax.rem(t + d, times), s), device_id_type=MESH)

    lanes = [pl.ds(i * LANES, LANES) for i in range(blocks)]
    for k in range(2):
        for i in range(blocks):
            pltpu.make_async_copy(
                c_ref.at[k, :, :, lanes[i]], ext.at[k, :, i, pl.ds(HALO, rows), :], local_sem.at[k]
            ).start()
    opening = pltpu.make_async_copy(c_ref.at[0], updated.at[0], local_sem.at[2])

    @pl.when(t == 0)
    def _():
        opening.start()

    pl.semaphore_wait(barrier, times + 1)

    def halo_copy(side, k, source, target):
        return pltpu.make_async_remote_copy(
            src_ref=source, dst_ref=target, send_sem=halo_send.at[side, k], recv_sem=halo_recv.at[side, k],
            device_id=(t, low if side else high), device_id_type=MESH,
        )

    for k in range(2):
        for i in range(blocks):
            for side, source, place in ((0, rows - HALO, 0), (1, 0, HALO + rows)):
                halo_copy(
                    side, k,
                    c_ref.at[k, :, pl.ds(source, HALO), lanes[i]],
                    ext.at[k, :, i, pl.ds(place, HALO), :],
                ).start()

    def halo_bytes(side, k):
        part = ext.at[k, :, :, pl.ds(0, HALO), :]
        return pltpu.make_async_remote_copy(
            src_ref=part, dst_ref=part, send_sem=halo_send.at[side, k], recv_sem=halo_recv.at[side, k],
            device_id=(t, high), device_id_type=MESH,
        )

    def propagate(load, count):
        a = states.at[0, :, pl.ds(0, count)]
        b = states.at[1, :, pl.ds(0, count)]
        for f in range(3):
            for r in range(count):
                for i in range(blocks):
                    value = load(f, i, r, count)
                    a[f, r, :, i * LANES:(i + 1) * LANES] = value if f == 0 else value * MOMENTUM_SCALE

        def two(_, square):
            step_rows(a, b, square)
            square = square * 0.25
            step_rows(b, a, square)
            return square * 0.25

        lax.fori_loop(0, FACTOR // 2, two, SQUARE_SCALE)
        return lambda f, i, r: a[f, r, :, i * LANES:(i + 1) * LANES] * SCALE_BACK[f]

    flip = (lax.rem(s, RUN) == 0).astype(jnp.int32)
    center = pl.ds(HALO, half)
    wrapped = t == times - 1

    def own_copy(w, offset):
        return [
            pltpu.make_async_copy(
                settled.at[w, 0, :, i, center, :], updated.at[1, :, pl.ds(offset, half), lanes[i]], local_sem.at[3]
            )
            for i in range(blocks)
        ]

    def back_copy(w):
        return pltpu.make_async_remote_copy(
            src_ref=settled.at[w, 0, :, :, center, :], dst_ref=behind.at[w, :, :, pl.ds(FACTOR, half), :],
            send_sem=back_send.at[w], recv_sem=back_recv.at[w], device_id=(before, s), device_id_type=MESH,
        )

    def on_copy(w, offset):
        return [
            pltpu.make_async_remote_copy(
                src_ref=settled.at[w, 1, :, i, center, :], dst_ref=updated.at[0, :, pl.ds(offset, half), lanes[i]],
                send_sem=on_send, recv_sem=on_recv, device_id=(after, s), device_id_type=MESH,
            )
            for i in range(blocks)
        ]

    def send_rows(w, k, offset):
        place = coarse.at[pl.ds(lax.rem(2 * t + 1 + k, 2 * times) * 3, 3)]

        @pl.loop(0, half)
        def _(d):
            row = lax.rem(t + d, half)
            j = offset + row
            source = stage.at[w, k, pl.ds((FACTOR + row) * 3, 3)]

            @pl.when(j != t)
            def _():
                pltpu.make_async_remote_copy(
                    src_ref=source, dst_ref=place, send_sem=row_send.at[k], recv_sem=row_recv.at[k],
                    device_id=(j, s), device_id_type=MESH,
                ).start()

            @pl.when(j == t)
            def _():
                pltpu.make_async_copy(source, place, local_sem.at[4 + k]).start()

    @pl.loop(0, 2)
    def _(w):
        side = lax.rem(w + flip, 2)
        offset = pl.multiple_of(side * half, SUBLANES)

        def advance(k):
            @pl.when(w == 0)
            def _():
                part = ext.at[k, :, :, pl.ds(HALO, rows), :]
                pltpu.make_async_copy(part, part, local_sem.at[k]).wait()

            halo_bytes(side, k).wait_recv()
            result = propagate(
                lambda f, i, r, count: ext[k, f, i, pl.ds(offset + r, SUBLANES, stride=count), :],
                wide // SUBLANES,
            )
            for f in range(3):
                for r in range(wide // SUBLANES):
                    for i in range(blocks):
                        settled[w, k, f, i, pl.ds(r, SUBLANES, stride=wide // SUBLANES), :] = result(f, i, r)

        def push(k):
            return propagate(
                lambda f, i, r, count: settled[w, k, f, i, pl.ds(FACTOR + r, SUBLANES, stride=count), :],
                narrow // SUBLANES,
            )

        def residual(k, result):
            count = narrow // SUBLANES
            for f in range(3):
                for r in range(count):
                    for i in range(blocks):
                        value = result(f, i, r)
                        if k == 0:
                            known = settled[w, 1, f, i, pl.ds(FACTOR + r, SUBLANES, stride=count), :]
                        else:
                            known = behind[w, f, i, pl.ds(r, SUBLANES, stride=count), :]
                            value = jnp.where(wrapped, known, value)
                        stage[w, k, pl.ds(r * 3 + f, SUBLANES, stride=3 * count), i, :] = value - known

        advance(0)
        back_copy(w).start()
        for copy in own_copy(w, offset):
            copy.start()
        result = push(0)
        for f in range(3):
            for r in range(narrow // SUBLANES):
                for i in range(blocks):
                    pushed_value = result(f, i, r)
                    stage[w, 0, pl.ds(r * 3 + f, SUBLANES, stride=3 * (narrow // SUBLANES)), i, :] = pushed_value
        advance(1)

        @pl.when(t < times - 1)
        def _():
            for copy in on_copy(w, offset):
                copy.start()

        count = narrow // SUBLANES
        residual(0, lambda f, i, r: stage[w, 0, pl.ds(r * 3 + f, SUBLANES, stride=3 * count), i, :])
        send_rows(w, 0, offset)
        result = push(1)
        back_copy(w).wait_recv()
        residual(1, result)
        send_rows(w, 1, offset)

    for k in range(2):
        for side in range(2):
            halo_bytes(side, k).wait_send()
    for w in range(2):
        back_copy(w).wait_send()
    pltpu.make_async_copy(updated.at[1], updated.at[1], local_sem.at[3]).wait()
    whole = pltpu.make_async_remote_copy(
        src_ref=updated.at[0], dst_ref=updated.at[0], send_sem=on_send, recv_sem=on_recv,
        device_id=(after, s), device_id_type=MESH,
    )

    @pl.when(t == 0)
    def _():
        opening.wait()

    @pl.when(t > 0)
    def _():
        whole.wait_recv()

    @pl.when(t < times - 1)
    def _():
        whole.wait_send()

    for k in range(2):
        part = coarse.at[pl.ds(0, 3 * (times - 1))]
        total = pltpu.make_async_remote_copy(
            src_ref=part, dst_ref=part, send_sem=row_send.at[k], recv_sem=row_recv.at[k],
            device_id=(after, s), device_id_type=MESH,
        )
        total.wait_recv()
        total.wait_send()
        one = coarse.at[pl.ds(0, 3)]
        pltpu.make_async_copy(one, one, local_sem.at[4 + k]).wait()


def solution(mesh):
    def on_device(c_points):
        intervals, fields, rows, columns = c_points.shape
        times = lax.axis_size("tm")
        blocks = columns // LANES
        full = rows + 2 * HALO
        wide = rows // 2 + 2 * HALO
        narrow = rows // 2 + 2 * FACTOR
        f32 = jnp.float32
        updated, coarse = pl.pallas_call(
            kernel,
            out_shape=(
                pltpu.VMEM(c_points.shape, f32),
                pltpu.VMEM((2 * times * fields, blocks, LANES), f32),
            ),
            in_specs=[pl.BlockSpec(memory_space=pl.ANY)],
            out_specs=(pl.BlockSpec(memory_space=pltpu.VMEM), pl.BlockSpec(memory_space=pltpu.VMEM)),
            scratch_shapes=[
                pltpu.VMEM((2, fields, blocks, full, LANES), f32),
                pltpu.VMEM((2, fields, wide // SUBLANES, SUBLANES, columns), f32),
                pltpu.VMEM((2, 2, fields, blocks, wide, LANES), f32),
                pltpu.VMEM((2, fields, blocks, narrow, LANES), f32),
                pltpu.VMEM((2, 2, narrow * fields, blocks, LANES), f32),
                pltpu.SemaphoreType.DMA((6,)),
                pltpu.SemaphoreType.DMA((2, 2)),
                pltpu.SemaphoreType.DMA((2, 2)),
                pltpu.SemaphoreType.DMA((2,)),
                pltpu.SemaphoreType.DMA((2,)),
                pltpu.SemaphoreType.DMA,
                pltpu.SemaphoreType.DMA,
                pltpu.SemaphoreType.DMA((2,)),
                pltpu.SemaphoreType.DMA((2,)),
            ],
            compiler_params=pltpu.CompilerParams(collective_id=0, has_side_effects=True),
        )(c_points)
        return updated, coarse.reshape(2 * times, fields, 1, 1, columns)

    return jax.shard_map(
        on_device,
        mesh=mesh,
        in_specs=(P("tm", None, "space", None),),
        out_specs=(P("tm", None, "space", None), P(None, None, "space", "tm", None)),
        check_vma=False,
    )
```

time: 43.4 us -> 39.7 us (0.915)
  Pallas kernels: 40.1 us -> 37.5 us
  local copies, waits for them, and re-layouts: 2.58 us -> 1.49 us
    pallas_call x1, Pallas kernels: 40.1 us -> 37.5 us  [on_device(): pl.pallas_call(kernel, out_shape=(pltpu.VMEM(c_points.shape, f32), pltpu....]
    unnamed x4 -> x2, local copies, waits for them, and re-layouts: 2.58 us -> 1.49 us
where the time goes in v2:
time: 39.7 us; the launch traced here: 39.6 us
  Pallas kernels  37.5 us (94%)
  local copies, waits for them, and re-layouts  1.49 us (4%)
  between operations  0.64 us (2%)
    pallas_call x1, Pallas kernels, on_device(): pl.pallas_call(kernel, out_shape=(pltpu.VMEM(c_points.shape, f32), pltpu....  37.5 us
    unnamed x2, local copies, waits for them, and re-layouts  1.49 us

profile of v2, /device:TPU:1, one launch (start us, length us, event | category | flops | bytes accessed | tf_op | source)
XLA Modules:
  0.0 39.6 jit_solution(15069083195574934307)
XLA Ops:
  0.6 37.5 %shard_map.30 = (f32[2,3,32,512]{3,2,1,0:T(8,128)S(1)}, f32[192,4,128]{2,1,0:T(4,128)S(1)}) custom-call(f32[2,3,32,512]{3,2,1,0:T(8,128)} %c_ref.1), custom_call_target="tpu_custom_call" | custom-call | tf_op jit(solution)/shard_map/pallas_call | solution.py:295
  38.1 0.7 %copy.7 = f32[2,3,32,512]{3,2,1,0:T(8,128)} copy(f32[2,3,32,512]{3,2,1,0:T(8,128)S(1)} %get-tuple-element.10) | data formatting | bytes 786432
  38.9 0.7 %copy.8 = f32[64,3,1,1,512]{4,3,2,1,0:T(1,128)} copy(f32[64,3,1,1,512]{4,3,2,1,0:T(1,128)S(1)} %bitcast.1) | data formatting | bytes 786432

commit v3 on v2

--- a/solution.py
+++ b/solution.py
@@ -13,6 +13,8 @@
 SQUARE_SCALE = 0.08
 SCALE_BACK = [0.25 ** FACTOR, 0.25 ** FACTOR / MOMENTUM_SCALE, 0.25 ** FACTOR / MOMENTUM_SCALE]
 RUN = 4
+LINE = 4
+CORES = 2
 MESH = pl.DeviceIdType.MESH
 
 
@@ -58,8 +60,9 @@
     put(0, first[0], second[1], [pltpu.roll(x, 1, axis=0) for x in old[2]])
 
 
-def kernel(c_ref, updated, coarse, ext, states, settled, behind, stage,
-           local_sem, halo_send, halo_recv, back_send, back_recv, on_send, on_recv, row_send, row_recv):
+def kernel(c_ref, updated, coarse, ext, relay, states, settled, behind, stage,
+           local_sem, halo_send, halo_recv, back_send, back_recv, on_send, on_recv, row_send, row_recv,
+           relay_send, relay_recv, known_in):
     t = lax.axis_index("tm")
     s = lax.axis_index("space")
     times = lax.axis_size("tm")
@@ -74,13 +77,53 @@
     before = lax.rem(t + times - 1, times)
     after = lax.rem(t + 1, times)
 
+    spot = lax.rem(s, RUN)
+    ending = spot == RUN - 1
+    starting = spot == 0
+    outer = jnp.logical_or(ending, starting)
+    inner = jnp.logical_not(outer)
+    upward = (spot < 2).astype(jnp.int32)
+    leads = jnp.logical_and(outer, s < strips // 2)
+    follows = jnp.logical_and(outer, s >= strips // 2)
+    distant = jnp.where(upward == 1, low, high)
+    beyond = lax.rem(s + strips + 2 - 4 * upward, strips)
+
+    plane = LINE * CORES
+    place_in_line = lax.rem(t // CORES, LINE)
+    partner = t + 1 - 2 * lax.rem(t, CORES)
+    around = (lax.rem(t + plane, times), lax.rem(t + times - plane, times))
+    fore = place_in_line < LINE - 1
+    aft = place_in_line > 0
+    along = 1 + jnp.logical_and(fore, aft).astype(jnp.int32)
+    near_pair = t + CORES * (1 - 2 * lax.rem(place_in_line, 2))
+    far_pair = t + 2 * CORES * (1 - 2 * (place_in_line // 2))
+
+    def tell(semaphore, group, strip=s):
+        pl.semaphore_signal(semaphore, inc=1, device_id=(group, strip), device_id_type=MESH)
+
+    def tell_around(semaphore):
+        for group in around:
+            tell(semaphore, group)
+
+        @pl.when(fore)
+        def _():
+            tell(semaphore, t + CORES)
+
+        @pl.when(aft)
+        def _():
+            tell(semaphore, t - CORES)
+
     barrier = pltpu.get_barrier_semaphore()
-    for neighbour in (low, high):
-        pl.semaphore_signal(barrier, inc=1, device_id=(t, neighbour), device_id_type=MESH)
-
-    @pl.loop(1, times)
-    def _(d):
-        pl.semaphore_signal(barrier, inc=1, device_id=(lax.rem(t + d, times), s), device_id_type=MESH)
+    @pl.when(jnp.logical_not(jnp.logical_and(follows, upward == 1)))
+    def _():
+        tell(barrier, t, low)
+
+    @pl.when(jnp.logical_not(jnp.logical_and(follows, upward == 0)))
+    def _():
+        tell(barrier, t, high)
+
+    tell(barrier, partner)
+    tell_around(barrier)
 
     lanes = [pl.ds(i * LANES, LANES) for i in range(blocks)]
     for k in range(2):
@@ -94,7 +137,7 @@
     def _():
         opening.start()
 
-    pl.semaphore_wait(barrier, times + 1)
+    pl.semaphore_wait(barrier, 5 + along - leads.astype(jnp.int32))
 
     def halo_copy(side, k, source, target):
         return pltpu.make_async_remote_copy(
@@ -102,14 +145,71 @@
             device_id=(t, low if side else high), device_id_type=MESH,
         )
 
+    def halo_start(side, k, source, place):
+        for i in range(blocks):
+            halo_copy(
+                side, k,
+                c_ref.at[k, :, pl.ds(source, HALO), lanes[i]],
+                ext.at[k, :, i, pl.ds(place, HALO), :],
+            ).start()
+
+    def side_start(side, k):
+        halo_start(side, k, 0 if side else rows - HALO, HALO + rows if side else 0)
+
+    def far_start():
+        relay_start()
+        for side in range(2):
+
+            @pl.when(upward == side)
+            def _():
+                side_start(side, 0)
+
+    def relay_start():
+        source = pl.multiple_of((1 - upward) * (rows - HALO), SUBLANES)
+        hop = jnp.where(upward == 1, high, low)
+        for i in range(blocks):
+            pltpu.make_async_remote_copy(
+                src_ref=c_ref.at[1, :, pl.ds(source, HALO), lanes[i]], dst_ref=relay.at[:, i],
+                send_sem=halo_send.at[upward, 1], recv_sem=relay_recv,
+                device_id=(t, hop), device_id_type=MESH,
+            ).start()
+
+    @pl.when(follows)
+    def _():
+        tell(known_in.at[4], t, distant)
+        far_start()
+
     for k in range(2):
-        for i in range(blocks):
-            for side, source, place in ((0, rows - HALO, 0), (1, 0, HALO + rows)):
-                halo_copy(
-                    side, k,
-                    c_ref.at[k, :, pl.ds(source, HALO), lanes[i]],
-                    ext.at[k, :, i, pl.ds(place, HALO), :],
-                ).start()
+        for side in range(2):
+
+            @pl.when(jnp.logical_or(inner, upward != side))
+            def _():
+                side_start(side, k)
+
+    def relay_copy():
+        place = pl.multiple_of(upward * (HALO + rows), SUBLANES)
+        return pltpu.make_async_remote_copy(
+            src_ref=relay, dst_ref=ext.at[1, :, :, pl.ds(place, HALO), :],
+            send_sem=relay_send, recv_sem=halo_recv.at[upward, 1],
+            device_id=(t, beyond), device_id_type=MESH,
+        )
+
+    tell_around(known_in.at[0])
+    pl.semaphore_wait(known_in.at[0], 2 + along)
+    for stage_index, group in ((1, near_pair), (2, far_pair), (3, partner)):
+        tell(known_in.at[stage_index], group)
+        pl.semaphore_wait(known_in.at[stage_index], 1)
+
+    def forward():
+        pltpu.make_async_remote_copy(
+            src_ref=relay, dst_ref=relay, send_sem=relay_send, recv_sem=relay_recv,
+            device_id=(t, high), device_id_type=MESH,
+        ).wait_recv()
+        relay_copy().start()
+
+    @pl.when(jnp.logical_and(inner, s >= strips // 2))
+    def _():
+        forward()
 
     def halo_bytes(side, k):
         part = ext.at[k, :, :, pl.ds(0, HALO), :]
@@ -136,7 +236,6 @@
         lax.fori_loop(0, FACTOR // 2, two, SQUARE_SCALE)
         return lambda f, i, r: a[f, r, :, i * LANES:(i + 1) * LANES] * SCALE_BACK[f]
 
-    flip = (lax.rem(s, RUN) == 0).astype(jnp.int32)
     center = pl.ds(HALO, half)
     wrapped = t == times - 1
 
@@ -185,7 +284,7 @@
 
     @pl.loop(0, 2)
     def _(w):
-        side = lax.rem(w + flip, 2)
+        side = lax.rem(w + upward, 2)
         offset = pl.multiple_of(side * half, SUBLANES)
 
         def advance(k):
@@ -223,7 +322,17 @@
                             value = jnp.where(wrapped, known, value)
                         stage[w, k, pl.ds(r * 3 + f, SUBLANES, stride=3 * count), i, :] = value - known
 
+        @pl.when(jnp.logical_and(w == 1, jnp.logical_and(inner, s < strips // 2)))
+        def _():
+            forward()
+
         advance(0)
+
+        @pl.when(jnp.logical_and(w == 0, leads))
+        def _():
+            pl.semaphore_wait(known_in.at[4], 1)
+            far_start()
+
         back_copy(w).start()
         for copy in own_copy(w, offset):
             copy.start()
@@ -233,6 +342,7 @@
                 for i in range(blocks):
                     pushed_value = result(f, i, r)
                     stage[w, 0, pl.ds(r * 3 + f, SUBLANES, stride=3 * (narrow // SUBLANES)), i, :] = pushed_value
+
         advance(1)
 
         @pl.when(t < times - 1)
@@ -253,6 +363,11 @@
             halo_bytes(side, k).wait_send()
     for w in range(2):
         back_copy(w).wait_send()
+
+    @pl.when(inner)
+    def _():
+        relay_copy().wait_send()
+
     pltpu.make_async_copy(updated.at[1], updated.at[1], local_sem.at[3]).wait()
     whole = pltpu.make_async_remote_copy(
         src_ref=updated.at[0], dst_ref=updated.at[0], send_sem=on_send, recv_sem=on_recv,
@@ -302,6 +417,7 @@
             out_specs=(pl.BlockSpec(memory_space=pltpu.VMEM), pl.BlockSpec(memory_space=pltpu.VMEM)),
             scratch_shapes=[
                 pltpu.VMEM((2, fields, blocks, full, LANES), f32),
+                pltpu.VMEM((fields, blocks, HALO, LANES), f32),
                 pltpu.VMEM((2, fields, wide // SUBLANES, SUBLANES, columns), f32),
                 pltpu.VMEM((2, 2, fields, blocks, wide, LANES), f32),
                 pltpu.VMEM((2, fields, blocks, narrow, LANES), f32),
@@ -315,6 +431,9 @@
                 pltpu.SemaphoreType.DMA,
                 pltpu.SemaphoreType.DMA((2,)),
                 pltpu.SemaphoreType.DMA((2,)),
+                pltpu.SemaphoreType.DMA,
+                pltpu.SemaphoreType.DMA,
+                pltpu.SemaphoreType.REGULAR((5,)),
             ],
             compiler_params=pltpu.CompilerParams(collective_id=0, has_side_effects=True),
         )(c_points)

time: 39.7 us -> 37.9 us (0.955)
  the two profiles are of different devices: /device:TPU:1 before, /device:TPU:225 now
where the time goes in v3:
time: 37.9 us; the launch traced here: 37.8 us
  Pallas kernels  35.7 us (94%)
  local copies, waits for them, and re-layouts  1.49 us (4%)
  between operations  0.64 us (2%)
    pallas_call x1, Pallas kernels, on_device(): pl.pallas_call(kernel, out_shape=(pltpu.VMEM(c_points.shape, f32), pltpu....  35.7 us
    unnamed x2, local copies, waits for them, and re-layouts  1.49 us

profile of v3, /device:TPU:225, one launch (start us, length us, event | category | flops | bytes accessed | tf_op | source)
XLA Modules:
  0.0 37.8 jit_solution(5514322481165592410)
XLA Ops:
  0.6 35.7 %shard_map.30 = (f32[2,3,32,512]{3,2,1,0:T(8,128)S(1)}, f32[192,4,128]{2,1,0:T(4,128)S(1)}) custom-call(f32[2,3,32,512]{3,2,1,0:T(8,128)} %c_ref.1), custom_call_target="tpu_custom_call" | custom-call | tf_op jit(solution)/shard_map/pallas_call | solution.py:410
  36.3 0.7 %copy.7 = f32[2,3,32,512]{3,2,1,0:T(8,128)} copy(f32[2,3,32,512]{3,2,1,0:T(8,128)S(1)} %get-tuple-element.10) | data formatting | bytes 786432
  37.1 0.7 %copy.8 = f32[64,3,1,1,512]{4,3,2,1,0:T(1,128)} copy(f32[64,3,1,1,512]{4,3,2,1,0:T(1,128)S(1)} %bitcast.1) | data formatting | bytes 786432

commit v4 on v3

--- a/solution.py
+++ b/solution.py
@@ -60,7 +60,7 @@
     put(0, first[0], second[1], [pltpu.roll(x, 1, axis=0) for x in old[2]])
 
 
-def kernel(c_ref, updated, coarse, ext, relay, states, settled, behind, stage,
+def kernel(c_ref, arrived, settled, coarse, ext, relay, states, pushed, behind, stage,
            local_sem, halo_send, halo_recv, back_send, back_recv, on_send, on_recv, row_send, row_recv,
            relay_send, relay_recv, known_in):
     t = lax.axis_index("tm")
@@ -131,11 +131,14 @@
             pltpu.make_async_copy(
                 c_ref.at[k, :, :, lanes[i]], ext.at[k, :, i, pl.ds(HALO, rows), :], local_sem.at[k]
             ).start()
-    opening = pltpu.make_async_copy(c_ref.at[0], updated.at[0], local_sem.at[2])
+    opening = [
+        pltpu.make_async_copy(c_ref.at[0, :, :, lanes[i]], arrived.at[:, i], local_sem.at[2]) for i in range(blocks)
+    ]
 
     @pl.when(t == 0)
     def _():
-        opening.start()
+        for copy in opening:
+            copy.start()
 
     pl.semaphore_wait(barrier, 5 + along - leads.astype(jnp.int32))
 
@@ -218,9 +221,9 @@
             device_id=(t, high), device_id_type=MESH,
         )
 
-    def propagate(load, count):
-        a = states.at[0, :, pl.ds(0, count)]
-        b = states.at[1, :, pl.ds(0, count)]
+    def propagate(load, count, buffers):
+        a = buffers.at[0, :, pl.ds(0, count)]
+        b = buffers.at[1, :, pl.ds(0, count)]
         for f in range(3):
             for r in range(count):
                 for i in range(blocks):
@@ -239,14 +242,6 @@
     center = pl.ds(HALO, half)
     wrapped = t == times - 1
 
-    def own_copy(w, offset):
-        return [
-            pltpu.make_async_copy(
-                settled.at[w, 0, :, i, center, :], updated.at[1, :, pl.ds(offset, half), lanes[i]], local_sem.at[3]
-            )
-            for i in range(blocks)
-        ]
-
     def back_copy(w):
         return pltpu.make_async_remote_copy(
             src_ref=settled.at[w, 0, :, :, center, :], dst_ref=behind.at[w, :, :, pl.ds(FACTOR, half), :],
@@ -254,33 +249,34 @@
         )
 
     def on_copy(w, offset):
-        return [
-            pltpu.make_async_remote_copy(
-                src_ref=settled.at[w, 1, :, i, center, :], dst_ref=updated.at[0, :, pl.ds(offset, half), lanes[i]],
-                send_sem=on_send, recv_sem=on_recv, device_id=(after, s), device_id_type=MESH,
-            )
-            for i in range(blocks)
-        ]
+        return pltpu.make_async_remote_copy(
+            src_ref=settled.at[w, 1, :, :, center, :], dst_ref=arrived.at[:, :, pl.ds(offset, half), :],
+            send_sem=on_send, recv_sem=on_recv, device_id=(after, s), device_id_type=MESH,
+        )
 
     def send_rows(w, k, offset):
         place = coarse.at[pl.ds(lax.rem(2 * t + 1 + k, 2 * times) * 3, 3)]
 
-        @pl.loop(0, half)
+        def row_copy(row):
+            return pltpu.make_async_remote_copy(
+                src_ref=stage.at[w, k, pl.ds((FACTOR + row) * 3, 3)], dst_ref=place,
+                send_sem=row_send.at[k], recv_sem=row_recv.at[k],
+                device_id=(offset + row, s), device_id_type=MESH,
+            )
+
+        @pl.loop(1, half)
         def _(d):
-            row = lax.rem(t + d, half)
-            j = offset + row
-            source = stage.at[w, k, pl.ds((FACTOR + row) * 3, 3)]
-
-            @pl.when(j != t)
-            def _():
-                pltpu.make_async_remote_copy(
-                    src_ref=source, dst_ref=place, send_sem=row_send.at[k], recv_sem=row_recv.at[k],
-                    device_id=(j, s), device_id_type=MESH,
-                ).start()
-
-            @pl.when(j == t)
-            def _():
-                pltpu.make_async_copy(source, place, local_sem.at[4 + k]).start()
+            row_copy(lax.rem(t + d, half)).start()
+
+        last = lax.rem(t, half)
+
+        @pl.when(offset + last != t)
+        def _():
+            row_copy(last).start()
+
+        @pl.when(offset + last == t)
+        def _():
+            pltpu.make_async_copy(stage.at[w, k, pl.ds((FACTOR + last) * 3, 3)], place, local_sem.at[3 + k]).start()
 
     @pl.loop(0, 2)
     def _(w):
@@ -296,17 +292,17 @@
             halo_bytes(side, k).wait_recv()
             result = propagate(
                 lambda f, i, r, count: ext[k, f, i, pl.ds(offset + r, SUBLANES, stride=count), :],
-                wide // SUBLANES,
+                wide // SUBLANES, states,
             )
             for f in range(3):
                 for r in range(wide // SUBLANES):
                     for i in range(blocks):
-                        settled[w, k, f, i, pl.ds(r, SUBLANES, stride=wide // SUBLANES), :] = result(f, i, r)
-
-        def push(k):
+                        settled[side, k, f, i, pl.ds(r, SUBLANES, stride=wide // SUBLANES), :] = result(f, i, r)
+
+        def push(k, buffers):
             return propagate(
-                lambda f, i, r, count: settled[w, k, f, i, pl.ds(FACTOR + r, SUBLANES, stride=count), :],
-                narrow // SUBLANES,
+                lambda f, i, r, count: settled[side, k, f, i, pl.ds(FACTOR + r, SUBLANES, stride=count), :],
+                narrow // SUBLANES, buffers,
             )
 
         def residual(k, result):
@@ -316,11 +312,11 @@
                     for i in range(blocks):
                         value = result(f, i, r)
                         if k == 0:
-                            known = settled[w, 1, f, i, pl.ds(FACTOR + r, SUBLANES, stride=count), :]
+                            known = settled[side, 1, f, i, pl.ds(FACTOR + r, SUBLANES, stride=count), :]
                         else:
-                            known = behind[w, f, i, pl.ds(r, SUBLANES, stride=count), :]
+                            known = behind[side, f, i, pl.ds(r, SUBLANES, stride=count), :]
                             value = jnp.where(wrapped, known, value)
-                        stage[w, k, pl.ds(r * 3 + f, SUBLANES, stride=3 * count), i, :] = value - known
+                        stage[side, k, pl.ds(r * 3 + f, SUBLANES, stride=3 * count), i, :] = value - known
 
         @pl.when(jnp.logical_and(w == 1, jnp.logical_and(inner, s < strips // 2)))
         def _():
@@ -333,30 +329,20 @@
             pl.semaphore_wait(known_in.at[4], 1)
             far_start()
 
-        back_copy(w).start()
-        for copy in own_copy(w, offset):
-            copy.start()
-        result = push(0)
-        for f in range(3):
-            for r in range(narrow // SUBLANES):
-                for i in range(blocks):
-                    pushed_value = result(f, i, r)
-                    stage[w, 0, pl.ds(r * 3 + f, SUBLANES, stride=3 * (narrow // SUBLANES)), i, :] = pushed_value
-
+        back_copy(side).start()
+        first = push(0, pushed)
         advance(1)
 
         @pl.when(t < times - 1)
         def _():
-            for copy in on_copy(w, offset):
-                copy.start()
-
-        count = narrow // SUBLANES
-        residual(0, lambda f, i, r: stage[w, 0, pl.ds(r * 3 + f, SUBLANES, stride=3 * count), i, :])
-        send_rows(w, 0, offset)
-        result = push(1)
-        back_copy(w).wait_recv()
-        residual(1, result)
-        send_rows(w, 1, offset)
+            on_copy(side, offset).start()
+
+        residual(0, first)
+        send_rows(side, 0, offset)
+        second = push(1, states)
+        back_copy(side).wait_recv()
+        residual(1, second)
+        send_rows(side, 1, offset)
 
     for k in range(2):
         for side in range(2):
@@ -368,15 +354,14 @@
     def _():
         relay_copy().wait_send()
 
-    pltpu.make_async_copy(updated.at[1], updated.at[1], local_sem.at[3]).wait()
     whole = pltpu.make_async_remote_copy(
-        src_ref=updated.at[0], dst_ref=updated.at[0], send_sem=on_send, recv_sem=on_recv,
+        src_ref=arrived, dst_ref=arrived, send_sem=on_send, recv_sem=on_recv,
         device_id=(after, s), device_id_type=MESH,
     )
 
     @pl.when(t == 0)
     def _():
-        opening.wait()
+        pltpu.make_async_copy(arrived, arrived, local_sem.at[2]).wait()
 
     @pl.when(t > 0)
     def _():
@@ -395,7 +380,22 @@
         total.wait_recv()
         total.wait_send()
         one = coarse.at[pl.ds(0, 3)]
-        pltpu.make_async_copy(one, one, local_sem.at[4 + k]).wait()
+        pltpu.make_async_copy(one, one, local_sem.at[3 + k]).wait()
+
+
+def place_outputs(arrived, settled, coarse, updated, rows_out, sem):
+    half = updated.shape[2] // 2
+    for i in range(arrived.shape[1]):
+        lane = pl.ds(i * LANES, LANES)
+        pltpu.make_async_copy(arrived.at[:, i], updated.at[0, :, :, lane], sem.at[0]).start()
+        for side in range(2):
+            pltpu.make_async_copy(
+                settled.at[side, 0, :, i, pl.ds(HALO, half), :], updated.at[1, :, pl.ds(side * half, half), lane], sem.at[0]
+            ).start()
+    rows = pltpu.make_async_copy(coarse, rows_out, sem.at[1])
+    rows.start()
+    pltpu.make_async_copy(updated, updated, sem.at[0]).wait()
+    rows.wait()
 
 
 def solution(mesh):
@@ -407,22 +407,23 @@
         wide = rows // 2 + 2 * HALO
         narrow = rows // 2 + 2 * FACTOR
         f32 = jnp.float32
-        updated, coarse = pl.pallas_call(
+        arrived, settled, coarse = pl.pallas_call(
             kernel,
             out_shape=(
-                pltpu.VMEM(c_points.shape, f32),
+                pltpu.VMEM((fields, blocks, rows, LANES), f32),
+                pltpu.VMEM((2, 2, fields, blocks, wide, LANES), f32),
                 pltpu.VMEM((2 * times * fields, blocks, LANES), f32),
             ),
             in_specs=[pl.BlockSpec(memory_space=pl.ANY)],
-            out_specs=(pl.BlockSpec(memory_space=pltpu.VMEM), pl.BlockSpec(memory_space=pltpu.VMEM)),
+            out_specs=(pl.BlockSpec(memory_space=pltpu.VMEM),) * 3,
             scratch_shapes=[
                 pltpu.VMEM((2, fields, blocks, full, LANES), f32),
                 pltpu.VMEM((fields, blocks, HALO, LANES), f32),
                 pltpu.VMEM((2, fields, wide // SUBLANES, SUBLANES, columns), f32),
-                pltpu.VMEM((2, 2, fields, blocks, wide, LANES), f32),
+                pltpu.VMEM((2, fields, narrow // SUBLANES, SUBLANES, columns), f32),
                 pltpu.VMEM((2, fields, blocks, narrow, LANES), f32),
                 pltpu.VMEM((2, 2, narrow * fields, blocks, LANES), f32),
-                pltpu.SemaphoreType.DMA((6,)),
+                pltpu.SemaphoreType.DMA((5,)),
                 pltpu.SemaphoreType.DMA((2, 2)),
                 pltpu.SemaphoreType.DMA((2, 2)),
                 pltpu.SemaphoreType.DMA((2,)),
@@ -437,6 +438,13 @@
             ],
             compiler_params=pltpu.CompilerParams(collective_id=0, has_side_effects=True),
         )(c_points)
+        updated, coarse = pl.pallas_call(
+            place_outputs,
+            out_shape=(jax.ShapeDtypeStruct(c_points.shape, f32), jax.ShapeDtypeStruct(coarse.shape, f32)),
+            in_specs=[pl.BlockSpec(memory_space=pl.ANY)] * 3,
+            out_specs=(pl.BlockSpec(memory_space=pl.ANY),) * 2,
+            scratch_shapes=[pltpu.SemaphoreType.DMA((2,))],
+        )(*(pltpu.with_memory_space_constraint(x, pltpu.VMEM) for x in (arrived, settled, coarse)))
         return updated, coarse.reshape(2 * times, fields, 1, 1, columns)
 
     return jax.shard_map(

time: 37.9 us -> 36.6 us (0.966)
  local copies, waits for them, and re-layouts: 1.49 us -> 0 us
    unnamed x2 -> x0, local copies, waits for them, and re-layouts: 1.49 us -> none
    pallas_call x1 -> x2, Pallas kernels: 35.7 us -> 35.9 us  [the longest x1 35 us: on_device(): pl.pallas_call(kernel, out_shape=(pltpu.VMEM((fields, blocks, rows, LANES...]
where the time goes in v4:
time: 36.6 us; the launch traced here: 36.5 us
  Pallas kernels  35.9 us (98%)
  between operations  0.64 us (2%)
    pallas_call x1, Pallas kernels, on_device(): pl.pallas_call(kernel, out_shape=(pltpu.VMEM((fields, blocks, rows, LANES...  35 us
    pallas_call x1, Pallas kernels, on_device(): pl.pallas_call(place_outputs, out_shape=(jax.ShapeDtypeStruct(c_points.sh...  0.89 us

profile of v4, /device:TPU:225, one launch (start us, length us, event | category | flops | bytes accessed | tf_op | source)
XLA Modules:
  0.0 36.5 jit_solution(10561408370434239112)
XLA Ops:
  0.6 35.0 %shard_map.30 = (f32[3,4,32,128]{3,2,1,0:T(8,128)S(1)}, f32[2,2,3,4,48,128]{5,4,3,2,1,0:T(8,128)S(1)}, f32[192,4,128]{2,1,0:T(4,128)S(1)}) custom-call(f32[2,3,32,512]{3,2,1,0:T(8,128)} %c_ref.1), custom_call_target="tpu_custom_call" | custom-call | tf_op jit(solution)/shard_map/pallas_call | solution.py:410
  35.7 0.9 %shard_map.31 = (f32[2,3,32,512]{3,2,1,0:T(8,128)}, f32[192,4,128]{2,1,0:T(4,128)}) custom-call(f32[3,4,32,128]{3,2,1,0:T(8,128)S(1)} %get-tuple-element.7.arrived, f32[2,2,3,4,48,128]{5,4,3,2,1,0:T(8,128)S(1)} %get-tuple-element.8.settled, f32[192,4,128]{2,1,0:T(4,128)S(1)} %get-tuple-element.9.coarse), custom_call_target="tpu_custom_call" | custom-call | tf_op jit(solution)/shard_map/pallas_call | solution.py:441

commit v5 on v4

--- a/solution.py
+++ b/solution.py
@@ -9,6 +9,7 @@
 LANES = 128
 HALO = 2 * FACTOR
 SUBLANES = 8
+UNROLL = 4
 MOMENTUM_SCALE = 0.4
 SQUARE_SCALE = 0.08
 SCALE_BACK = [0.25 ** FACTOR, 0.25 ** FACTOR / MOMENTUM_SCALE, 0.25 ** FACTOR / MOMENTUM_SCALE]
@@ -230,13 +231,13 @@
                     value = load(f, i, r, count)
                     a[f, r, :, i * LANES:(i + 1) * LANES] = value if f == 0 else value * MOMENTUM_SCALE
 
-        def two(_, square):
-            step_rows(a, b, square)
-            square = square * 0.25
-            step_rows(b, a, square)
-            return square * 0.25
-
-        lax.fori_loop(0, FACTOR // 2, two, SQUARE_SCALE)
+        def group(_, square):
+            for source, target in ((a, b), (b, a)) * (UNROLL // 2):
+                step_rows(source, target, square)
+                square = square * 0.25
+            return square
+
+        lax.fori_loop(0, FACTOR // UNROLL, group, SQUARE_SCALE)
         return lambda f, i, r: a[f, r, :, i * LANES:(i + 1) * LANES] * SCALE_BACK[f]
 
     center = pl.ds(HALO, half)
@@ -277,6 +278,11 @@
         @pl.when(offset + last == t)
         def _():
             pltpu.make_async_copy(stage.at[w, k, pl.ds((FACTOR + last) * 3, 3)], place, local_sem.at[3 + k]).start()
+
+    @pl.when(leads)
+    def _():
+        pl.semaphore_wait(known_in.at[4], 1)
+        far_start()
 
     @pl.loop(0, 2)
     def _(w):
@@ -318,16 +324,7 @@
                             value = jnp.where(wrapped, known, value)
                         stage[side, k, pl.ds(r * 3 + f, SUBLANES, stride=3 * count), i, :] = value - known
 
-        @pl.when(jnp.logical_and(w == 1, jnp.logical_and(inner, s < strips // 2)))
-        def _():
-            forward()
-
         advance(0)
-
-        @pl.when(jnp.logical_and(w == 0, leads))
-        def _():
-            pl.semaphore_wait(known_in.at[4], 1)
-            far_start()
 
         back_copy(side).start()
         first = push(0, pushed)
@@ -339,6 +336,10 @@
 
         residual(0, first)
         send_rows(side, 0, offset)
+        @pl.when(jnp.logical_and(w == 0, jnp.logical_and(inner, s < strips // 2)))
+        def _():
+            forward()
+
         second = push(1, states)
         back_copy(side).wait_recv()
         residual(1, second)

time: 36.6 us -> 35.9 us (0.981)
  the two profiles are of different devices: /device:TPU:225 before, /device:TPU:1 now
where the time goes in v5:
time: 35.9 us; the launch traced here: 35.2 us
  Pallas kernels  34.6 us (96%)
  between operations  0.64 us (2%)
    pallas_call x1, Pallas kernels, on_device(): pl.pallas_call(kernel, out_shape=(pltpu.VMEM((fields, blocks, rows, LANES...  33.7 us
    pallas_call x1, Pallas kernels, on_device(): pl.pallas_call(place_outputs, out_shape=(jax.ShapeDtypeStruct(c_points.sh...  0.89 us

profile of v5, /device:TPU:1, one launch (start us, length us, event | category | flops | bytes accessed | tf_op | source)
XLA Modules:
  0.0 35.2 jit_solution(8515106862517941407)
XLA Ops:
  0.6 33.7 %shard_map.30 = (f32[3,4,32,128]{3,2,1,0:T(8,128)S(1)}, f32[2,2,3,4,48,128]{5,4,3,2,1,0:T(8,128)S(1)}, f32[192,4,128]{2,1,0:T(4,128)S(1)}) custom-call(f32[2,3,32,512]{3,2,1,0:T(8,128)} %c_ref.1), custom_call_target="tpu_custom_call" | custom-call | tf_op jit(solution)/shard_map/pallas_call | solution.py:411
  34.4 0.9 %shard_map.31 = (f32[2,3,32,512]{3,2,1,0:T(8,128)}, f32[192,4,128]{2,1,0:T(4,128)}) custom-call(f32[3,4,32,128]{3,2,1,0:T(8,128)S(1)} %get-tuple-element.7.arrived, f32[2,2,3,4,48,128]{5,4,3,2,1,0:T(8,128)S(1)} %get-tuple-element.8.settled, f32[192,4,128]{2,1,0:T(4,128)S(1)} %get-tuple-element.9.coarse), custom_call_target="tpu_custom_call" | custom-call | tf_op jit(solution)/shard_map/pallas_call | solution.py:442

commit v6 on v5

--- a/solution.py
+++ b/solution.py
@@ -330,10 +330,6 @@
         first = push(0, pushed)
         advance(1)
 
-        @pl.when(t < times - 1)
-        def _():
-            on_copy(side, offset).start()
-
         residual(0, first)
         send_rows(side, 0, offset)
         @pl.when(jnp.logical_and(w == 0, jnp.logical_and(inner, s < strips // 2)))
@@ -344,6 +340,11 @@
         back_copy(side).wait_recv()
         residual(1, second)
         send_rows(side, 1, offset)
+
+        @pl.when(t < times - 1)
+        def _():
+            on_copy(side, offset).start()
+
 
     for k in range(2):
         for side in range(2):

time: 35.9 us -> 35.2 us (0.981)
  the two profiles are of different devices: /device:TPU:1 before, /device:TPU:3 now
where the time goes in v6:
time: 35.2 us; the launch traced here: 35.1 us
  Pallas kernels  34.5 us (98%)
  between operations  0.64 us (2%)
    pallas_call x1, Pallas kernels, on_device(): pl.pallas_call(kernel, out_shape=(pltpu.VMEM((fields, blocks, rows, LANES...  33.6 us
    pallas_call x1, Pallas kernels, on_device(): pl.pallas_call(place_outputs, out_shape=(jax.ShapeDtypeStruct(c_points.sh...  0.89 us

profile of v6, /device:TPU:3, one launch (start us, length us, event | category | flops | bytes accessed | tf_op | source)
XLA Modules:
  0.0 35.1 jit_solution(1573878636762173952)
XLA Ops:
  0.6 33.6 %shard_map.30 = (f32[3,4,32,128]{3,2,1,0:T(8,128)S(1)}, f32[2,2,3,4,48,128]{5,4,3,2,1,0:T(8,128)S(1)}, f32[192,4,128]{2,1,0:T(4,128)S(1)}) custom-call(f32[2,3,32,512]{3,2,1,0:T(8,128)} %c_ref.1), custom_call_target="tpu_custom_call" | custom-call | tf_op jit(solution)/shard_map/pallas_call | solution.py:412
  34.2 0.9 %shard_map.31 = (f32[2,3,32,512]{3,2,1,0:T(8,128)}, f32[192,4,128]{2,1,0:T(4,128)}) custom-call(f32[3,4,32,128]{3,2,1,0:T(8,128)S(1)} %get-tuple-element.7.arrived, f32[2,2,3,4,48,128]{5,4,3,2,1,0:T(8,128)S(1)} %get-tuple-element.8.settled, f32[192,4,128]{2,1,0:T(4,128)S(1)} %get-tuple-element.9.coarse), custom_call_target="tpu_custom_call" | custom-call | tf_op jit(solution)/shard_map/pallas_call | solution.py:443

commit v7 on v6

--- a/solution.py
+++ b/solution.py
@@ -341,10 +341,15 @@
         residual(1, second)
         send_rows(side, 1, offset)
 
-        @pl.when(t < times - 1)
+        @pl.when(jnp.logical_and(t < times - 1, outer))
         def _():
             on_copy(side, offset).start()
 
+
+    @pl.when(jnp.logical_and(t < times - 1, inner))
+    def _():
+        for side in range(2):
+            on_copy(side, side * half).start()
 
     for k in range(2):
         for side in range(2):

time: 35.2 us -> 34.4 us (0.977)
  the two profiles are of different devices: /device:TPU:3 before, /device:TPU:1 now
where the time goes in v7:
time: 34.4 us
  Pallas kernels  33.7 us (98%)
  between operations  0.64 us (2%)
    pallas_call x1, Pallas kernels, on_device(): pl.pallas_call(kernel, out_shape=(pltpu.VMEM((fields, blocks, rows, LANES...  32.8 us
    pallas_call x1, Pallas kernels, on_device(): pl.pallas_call(place_outputs, out_shape=(jax.ShapeDtypeStruct(c_points.sh...  0.89 us

profile of v7, /device:TPU:1, one launch (start us, length us, event | category | flops | bytes accessed | tf_op | source)
XLA Modules:
  0.0 34.4 jit_solution(8991329694242507959)
XLA Ops:
  0.6 32.8 %shard_map.30 = (f32[3,4,32,128]{3,2,1,0:T(8,128)S(1)}, f32[2,2,3,4,48,128]{5,4,3,2,1,0:T(8,128)S(1)}, f32[192,4,128]{2,1,0:T(4,128)S(1)}) custom-call(f32[2,3,32,512]{3,2,1,0:T(8,128)} %c_ref.1), custom_call_target="tpu_custom_call" | custom-call | tf_op jit(solution)/shard_map/pallas_call | solution.py:417
  33.5 0.9 %shard_map.31 = (f32[2,3,32,512]{3,2,1,0:T(8,128)}, f32[192,4,128]{2,1,0:T(4,128)}) custom-call(f32[3,4,32,128]{3,2,1,0:T(8,128)S(1)} %get-tuple-element.7.arrived, f32[2,2,3,4,48,128]{5,4,3,2,1,0:T(8,128)S(1)} %get-tuple-element.8.settled, f32[192,4,128]{2,1,0:T(4,128)S(1)} %get-tuple-element.9.coarse), custom_call_target="tpu_custom_call" | custom-call | tf_op jit(solution)/shard_map/pallas_call | solution.py:448

commit v8 on v7

--- a/solution.py
+++ b/solution.py
@@ -279,11 +279,6 @@
         def _():
             pltpu.make_async_copy(stage.at[w, k, pl.ds((FACTOR + last) * 3, 3)], place, local_sem.at[3 + k]).start()
 
-    @pl.when(leads)
-    def _():
-        pl.semaphore_wait(known_in.at[4], 1)
-        far_start()
-
     @pl.loop(0, 2)
     def _(w):
         side = lax.rem(w + upward, 2)
@@ -325,6 +320,12 @@
                         stage[side, k, pl.ds(r * 3 + f, SUBLANES, stride=3 * count), i, :] = value - known
 
         advance(0)
+
+        @pl.when(jnp.logical_and(w == 0, leads))
+        def _():
+            pl.semaphore_wait(known_in.at[4], 1)
+            far_start()
+
 
         back_copy(side).start()
         first = push(0, pushed)

time: 34.4 us -> 34.8 us (1.012)
  no operation moved by 1% of the time
where the time goes in v8:
time: 34.8 us; the launch traced here: 34.7 us
  Pallas kernels  34 us (98%)
  between operations  0.64 us (2%)
    pallas_call x1, Pallas kernels, on_device(): pl.pallas_call(kernel, out_shape=(pltpu.VMEM((fields, blocks, rows, LANES...  33.1 us
    pallas_call x1, Pallas kernels, on_device(): pl.pallas_call(place_outputs, out_shape=(jax.ShapeDtypeStruct(c_points.sh...  0.89 us

profile of v8, /device:TPU:1, one launch (start us, length us, event | category | flops | bytes accessed | tf_op | source)
XLA Modules:
  0.0 34.7 jit_solution(17422563356250134688)
XLA Ops:
  0.6 33.1 %shard_map.30 = (f32[3,4,32,128]{3,2,1,0:T(8,128)S(1)}, f32[2,2,3,4,48,128]{5,4,3,2,1,0:T(8,128)S(1)}, f32[192,4,128]{2,1,0:T(4,128)S(1)}) custom-call(f32[2,3,32,512]{3,2,1,0:T(8,128)} %c_ref.1), custom_call_target="tpu_custom_call" | custom-call | tf_op jit(solution)/shard_map/pallas_call | solution.py:418
  33.8 0.9 %shard_map.31 = (f32[2,3,32,512]{3,2,1,0:T(8,128)}, f32[192,4,128]{2,1,0:T(4,128)}) custom-call(f32[3,4,32,128]{3,2,1,0:T(8,128)S(1)} %get-tuple-element.7.arrived, f32[2,2,3,4,48,128]{5,4,3,2,1,0:T(8,128)S(1)} %get-tuple-element.8.settled, f32[192,4,128]{2,1,0:T(4,128)S(1)} %get-tuple-element.9.coarse), custom_call_target="tpu_custom_call" | custom-call | tf_op jit(solution)/shard_map/pallas_call | solution.py:449
